TPU v7x, 32 devices: a whole 2x2x4 slice. The times are simulated.
32 devices in a mesh: tm: 4 (over y, x), vox: 8 (over z, core).
Axes of the slice: x: 2, y: 2, z: 4, core: 2. Of those that a mesh axis runs over, the one named last changes fastest.
Arguments:
- u_train: bfloat16 [3072, 4096], P('tm'), may hold values from -0.109375 to 0.109375
- y_train: bfloat16 [3072, 3072], P('tm', 'vox'), may hold values from -6 to 6
- sing: float32 [4096], replicated, may hold values from 0.5 to 8
- lambdas: float32 [20], replicated, may hold values from 0.1 to 100
- lam_index: int32 [24], P('vox'), may hold values from 0 to 19
- live: int32 [24], P('vox'), may hold values from 0 to 1, as said below
- v_basis: bfloat16 [4096, 4096], P('tm', 'vox'), may hold values from -0.09375 to 0.09375
- x_test: bfloat16 [1024, 4096], P(None, 'tm'), may hold values from -0.09375 to 0.09375
Outputs:
- weights: bfloat16 [4096, 3072], P('tm', 'vox')
- predictions: bfloat16 [1024, 3072], P('tm', 'vox')
Inputs may be any that keep to these rules, and one draw needn't show every extreme that they name: Of the 3 voxel blocks that one device along vox holds, at most 2 are live, and some device holds exactly 2.
All inputs are finite; a program needn't handle non-finite values.
Results may differ from a plain program's by a relative error of at most 0.0058.
Values may be sent and summed in bfloat16 or wider, within the bound.
A program may use at most 128 MiB of HBM per device.

v0:
```python
import jax
import jax.numpy as jnp
from jax import lax
from jax.sharding import PartitionSpec as P

BLK = 128


def body(u_train, y_train, sing, lambdas, lam_index, live, v_basis, x_test):
    time_rows = y_train.shape[0]
    column_count = y_train.shape[1]
    block_count = lam_index.shape[0]
    penalty_count = lambdas.shape[0]
    capacity = block_count - block_count // 3
    selector = (lam_index[:, None] == jnp.arange(penalty_count, dtype=jnp.int32)[None, :]).astype(
        jnp.float32
    )
    selector = selector * live[:, None].astype(jnp.float32)
    ranking = jnp.argsort((1 - live) * block_count + jnp.arange(block_count, dtype=jnp.int32))
    picked = ranking[:capacity]
    responses = jnp.take(y_train.reshape(time_rows, block_count, BLK), picked, axis=1)
    responses = responses.reshape(time_rows, capacity * BLK)
    used_selector = jnp.take(selector, picked, axis=0)
    used_columns = responses.shape[1]
    used_blocks = used_selector.shape[0]
    partial_value = lax.dot_general(
        u_train, responses, (((0,), (0,)), ((), ())), preferred_element_type=jnp.float32
    )
    products = lax.psum(partial_value, "tm")
    filters = sing[None, :] / (sing[None, :] * sing[None, :] + lambdas[:, None])
    row_count = products.shape[0]
    blocks = (
        products.reshape(row_count, used_blocks, BLK)
        * jnp.dot(used_selector, filters, precision=lax.Precision.HIGHEST).T[:, :, None]
    )
    filtered = blocks.reshape(row_count, used_columns).astype(jnp.bfloat16)
    weight_sum = jnp.dot(
        lax.all_gather(v_basis, "vox", axis=1, tiled=True),
        filtered,
        preferred_element_type=jnp.float32,
    )
    weight_cols = weight_sum.astype(jnp.bfloat16)
    partial_test = jnp.dot(x_test, weight_cols, preferred_element_type=jnp.float32)
    predicted = lax.psum_scatter(partial_test, "tm", scatter_dimension=0, tiled=True).astype(
        jnp.bfloat16
    )

    def expand(values):
        row_count = values.shape[0]
        placed = jnp.zeros((row_count, block_count, BLK), values.dtype)
        placed = placed.at[:, picked, :].set(values.reshape(row_count, capacity, BLK))
        return placed.reshape(row_count, column_count)

    return (expand(weight_cols), expand(predicted))


def solution(mesh):
    placed = (
        P("tm", None),
        P("tm", "vox"),
        P(),
        P(),
        P("vox"),
        P("vox"),
        P("tm", "vox"),
        P(None, "tm"),
    )
    return jax.shard_map(
        body,
        mesh=mesh,
        in_specs=placed,
        out_specs=(P("tm", "vox"), P("tm", "vox")),
        check_vma=False,
    )
```

profile of v0, /device:TPU:0, one launch (start us, length us, event | category | flops | bytes accessed | tf_op | source)
XLA Modules:
  0.0 177.4 jit_solution(16627243049810682810)
XLA Ops:
  8.0 0.0 copy-start
  8.0 0.0 all-reduce.2.cloned.1.call-start
  8.1 0.8 fusion.10
  8.9 0.7 sort.17
  9.6 1.3 copy.20
  10.9 0.3 copy.21
  11.3 1.3 gather_fusion
  12.6 1.2 copy.22
  13.8 0.1 broadcast_bitcast_fusion
  13.8 0.1 bitcast_select_fusion
  14.0 6.6 %convolution_bitcast_fusion = f32[4096,256]{0,1:T(8,128)} fusion(bf16[768,256]{0,1:T(8,128)(2,1)S(1)} %bitcast_select_fusion, bf16[768,4096]{1,0:T(8,128)(2,1)} %param.8), kind=kOutput, calls=%fused_computation.4 | convolution fusion | flops 1610612736 | bytes 10878976 | tf_op jit(solution)/shard_map/dot_general | solution.py:26
  20.6 0.0 copy-start.2
  20.6 0.0 copy-start.1
  20.6 0.0 copy-start.3
  20.6 0.0 all-reduce.2.cloned.1.call-update
  20.6 0.0 all-gather.2.cloned.1.call-start
  20.7 0.5 all-gather.2.cloned.1.call-update
  21.2 0.0 reduce-scatter.2.cloned.1.call-start
  21.3 0.0 copy-done.2
  21.3 0.1 fusion.5
  21.3 0.6 gather_fusion.1
  21.9 0.0 copy-done.1
  21.9 0.0 copy-done.3
  21.9 0.5 fusion.1
  22.4 104.7 %all-reduce.2.cloned.1.call-done = f32[4096,256]{0,1:T(8,128)} async-done(((f32[4096,256]{0,1:T(8,128)}), f32[4096,256]{0,1:T(8,128)}) %all-reduce.2.cloned.1.call-update) | async-done | bytes 4194320 | tf_op jit(solution)/shard_map/psum | solution.py:29
  127.1 3.9 %fusion = bf16[4096,256]{0,1:T(8,128)(2,1)} fusion(f32[4096,256]{0,1:T(8,128)} %all-reduce.2.cloned.1.call-done, f32[4096,2]{0,1:T(2,128)S(1)} %fusion.1), kind=kLoop, calls=%fused_computation.6 | loop fusion | flops 2097152 | bytes 6324224 | tf_op jit(solution)/shard_map/convert_element_type | solution.py:36
  131.0 0.0 all-gather.2.cloned.1.call-done
  131.0 6.4 %convolution_convert_fusion = bf16[256,1024]{1,0:T(8,128)(2,1)S(1)} fusion(bf16[4096,256]{0,1:T(8,128)(2,1)} %fusion, bf16[1024,4096]{1,0:T(8,128)(2,1)} %all-gather.2.cloned.1.call-done), kind=kOutput, calls=%fused_computation.8 | convolution fusion | flops 2147745792 | bytes 11010048 | tf_op jit(solution)/shard_map/dot_general | solution.py:37
  137.4 0.0 copy-done
  137.4 1.7 convolution_bitcast_fusion.1
  139.1 0.0 reduce-scatter.2.cloned.1.call-update
  139.2 0.3 copy.23
  139.4 0.1 broadcast_in_dim.42
  139.6 0.7 scatter_fusion
  140.3 1.2 copy.24
  141.5 2.3 %copy.27 = bf16[1024,384]{1,0:T(8,128)(2,1)} copy(bf16[1024,384]{0,1:T(8,128)(2,1)} %bitcast.28) | data formatting | bytes 1572864
  143.8 23.4 %reduce-scatter.2.cloned.1.call-done = f32[256,256]{0,1:T(8,128)} async-done(((f32[1024,256]{0,1:T(8,128)}), f32[256,256]{0,1:T(8,128)}) %reduce-scatter.2.cloned.1.call-update) | async-done | bytes 262160 | tf_op jit(solution)/shard_map/reduce_scatter | solution.py:44
  167.3 1.0 convert_element_type.21
  168.2 0.1 copy.25
  168.4 0.6 scatter_fusion.1
  169.0 0.1 copy.26
  169.2 0.8 copy.28
  (5 shorter events, 0.0 us)
Async XLA Ops:
  8.0 129.4 %copy-start = (bf16[1024,1024]{1,0:T(8,128)(2,1)S(1)}, bf16[1024,1024]{1,0:T(8,128)(2,1)}, u32[]{:S(2)}) copy-start(bf16[1024,1024]{1,0:T(8,128)(2,1)} %param.15) | copy-start | bytes 6291460
  8.0 119.1 %all-reduce.2.cloned.1.call-start = ((), (), s32[]{:S(2)}) async-start(), calls=%async_computation.1 | async-start | bytes 8388608 | tf_op jit(solution)/shard_map/psum | solution.py:29
  20.6 0.7 copy-start.2
  20.6 1.3 copy-start.1
  20.6 1.3 copy-start.3
  20.6 110.4 %all-gather.2.cloned.1.call-start = ((), (), s32[]{:S(2)}) async-start(), calls=%async_computation.2 | async-start | bytes 9437184 | tf_op jit(solution)/shard_map/all_gather | solution.py:38
  21.2 146.1 %reduce-scatter.2.cloned.1.call-start = ((), (), s32[]{:S(2)}) async-start(), calls=%async_computation.3 | async-start | bytes 1310720 | tf_op jit(solution)/shard_map/reduce_scatter | solution.py:44
Sparse Core Ops, SparseCore 0:
  20.7 106.3 all-reduce.1
  139.3 27.9 reduce-scatter.1
Sparse Core Ops, SparseCore 1:
  22.7 84.6 all-gather.1
where the time goes:
time: 178 us; the launch traced here: 177 us
  waiting for transfers between devices  129 us (72%)
  between operations  15.6 us (9%)
  matrix products  15.2 us (9%)
  local copies, waits for them, and re-layouts  11.1 us (6%)
  other arithmetic  6.63 us (4%)
    psum x1, waiting for transfers between devices, body(): products = lax.psum(partial_value, 'tm')  105 us
    reduce_scatter x1, waiting for transfers between devices, body(): lax.psum_scatter(partial_test, 'tm', scatter_dimension=0, tiled=True)  23.4 us
    dot_general x1, matrix products, body(): lax.dot_general(u_train, responses, (((0,), (0,)), ((), ())), preferred_e...  6.63 us
    dot_general x1, matrix products, body(): jnp.dot(lax.all_gather(v_basis, 'vox', axis=1, tiled=True), filtered, pre...  6.38 us
    unnamed x11, local copies, waits for them, and re-layouts  4.43 us
    convert_element_type x1, other arithmetic, body(): filtered = blocks.reshape(row_count, used_columns).astype(jnp.bfloat16)  3.9 us
  transfers between devices with their start and end apart: 3, of which 2 were waited for; matrix products, arithmetic and copies ran while one was open for 5% of the time, Pallas kernels for 0%

commit v1 on v0

--- a/solution.py
+++ b/solution.py
@@ -26,7 +26,9 @@
     partial_value = lax.dot_general(
         u_train, responses, (((0,), (0,)), ((), ())), preferred_element_type=jnp.float32
     )
-    products = lax.psum(partial_value, "tm")
+    products = partial_value
+    for hop in (1, 2):
+        products = products + lax.ppermute(products, "tm", [(dev, dev ^ hop) for dev in range(4)])
     filters = sing[None, :] / (sing[None, :] * sing[None, :] + lambdas[:, None])
     row_count = products.shape[0]
     blocks = (

time: 178 us -> 260 us (1.46)
  waiting for transfers between devices: 129 us -> 205 us
  starting transfers between devices: 0.12 us -> 4.87 us
  other arithmetic: 6.63 us -> 10.7 us
    ppermute x0 -> x2, waiting for transfers between devices: none -> 180 us  [body(): lax.ppermute(products, 'tm', [(dev, dev ^ hop) for dev in range(4)])]
    psum x1 -> x0, waiting for transfers between devices: 105 us -> none  [body(): products = lax.psum(partial_value, 'tm')]
    ppermute x0 -> x2, starting transfers between devices: none -> 4.8 us  [body(): lax.ppermute(products, 'tm', [(dev, dev ^ hop) for dev in range(4)])]
  transfers between devices with their start and end apart: 3 -> 4, of which waited for: 2 -> 3; matrix products, arithmetic and copies ran while one was open for 5% -> 9% of each run, Pallas kernels for 0% -> 0%
where the time goes in v1:
time: 260 us; the launch traced here: 259 us
  waiting for transfers between devices  205 us (79%)
  between operations  14.2 us (5%)
  matrix products  13.3 us (5%)
  local copies, waits for them, and re-layouts  11.1 us (4%)
  other arithmetic  10.7 us (4%)
  starting transfers between devices  4.87 us (2%)
    ppermute x2, waiting for transfers between devices, body(): lax.ppermute(products, 'tm', [(dev, dev ^ hop) for dev in range(4)])  180 us
    reduce_scatter x1, waiting for transfers between devices, body(): lax.psum_scatter(partial_test, 'tm', scatter_dimension=0, tiled=True)  24.7 us
    dot_general x1, matrix products, body(): jnp.dot(lax.all_gather(v_basis, 'vox', axis=1, tiled=True), filtered, pre...  6.38 us
    convert_element_type x1, other arithmetic, body(): filtered = blocks.reshape(row_count, used_columns).astype(jnp.bfloat16)  5.58 us
  transfers between devices with their start and end apart: 4, of which 3 were waited for; matrix products, arithmetic and copies ran while one was open for 9% of the time, Pallas kernels for 0%

profile of v1, /device:TPU:0, one launch (start us, length us, event | category | flops | bytes accessed | tf_op | source)
XLA Modules:
  0.0 259.3 jit_solution(14724247237369869716)
XLA Ops:
  7.2 0.0 copy-start
  7.2 0.0 all-gather.2.cloned.1.call-start
  7.2 0.7 all-gather.2.cloned.1.call-update
  7.9 0.0 reduce-scatter.2.cloned.1.call-start
  8.0 1.3 copy.20
  9.3 0.3 copy.21
  9.6 0.7 fusion.10
  10.3 0.7 sort.17
  11.1 1.3 gather_fusion
  12.4 1.2 copy.22
  13.6 0.1 broadcast_bitcast_fusion
  13.7 0.1 bitcast_select_fusion
  13.8 4.7 %convolution_bitcast_fusion = f32[4096,256]{0,1:T(8,128)S(1)} fusion(bf16[768,256]{0,1:T(8,128)(2,1)S(1)} %bitcast_select_fusion, bf16[768,4096]{1,0:T(8,128)(2,1)} %param.8), kind=kOutput, calls=%fused_computation.4 | convolution fusion | flops 1610612736 | bytes 10878976 | tf_op jit(solution)/shard_map/dot_general | solution.py:26
  18.5 0.0 copy-start.2
  18.5 0.0 copy-start.1
  18.5 0.0 copy-start.3
  18.5 3.0 %collective-permute-start = (f32[4096,256]{0,1:T(8,128)S(1)}, f32[4096,256]{0,1:T(8,128)S(1)}, u32[]{:S(2)}, u32[]{:S(2)}) collective-permute-start(f32[4096,256]{0,1:T(8,128)S(1)} %convolution_bitcast_fusion), channel_id=1, source_target_pairs={{0,8},{8,0},{16,24},{24,16},{1,9},{9,1},{17,25},{25,17},{2,10},{10... | collective-permute-start | bytes 12582920 | tf_op jit(solution)/shard_map/ppermute | solution.py:31
  21.5 90.6 %collective-permute-done = f32[4096,256]{0,1:T(8,128)S(1)} collective-permute-done((f32[4096,256]{0,1:T(8,128)S(1)}, f32[4096,256]{0,1:T(8,128)S(1)}, u32[]{:S(2)}, u32[]{:S(2)}) %collective-permute-start) | collective-permute-done | bytes 4194336 | tf_op jit(solution)/shard_map/ppermute | solution.py:31
  112.1 2.5 add.34
  114.6 1.8 collective-permute-start.1
  116.3 0.0 copy-done.2
  116.3 0.1 fusion.5
  116.4 0.6 gather_fusion.1
  117.0 0.0 copy-done.1
  117.0 0.0 copy-done.3
  117.0 0.5 fusion.1
  117.5 89.1 %collective-permute-done.1 = f32[4096,256]{0,1:T(8,128)} collective-permute-done((f32[4096,256]{0,1:T(8,128)}, f32[4096,256]{0,1:T(8,128)}, u32[]{:S(2)}, u32[]{:S(2)}) %collective-permute-start.1) | collective-permute-done | bytes 4194336 | tf_op jit(solution)/shard_map/ppermute | solution.py:31
  206.6 5.6 %fusion = bf16[4096,256]{0,1:T(8,128)(2,1)} fusion(f32[4096,256]{0,1:T(8,128)} %add.34, f32[4096,256]{0,1:T(8,128)} %collective-permute-done.1, f32[4096,2]{0,1:T(2,128)S(1)} %fusion.1), kind=kLoop, calls=%fused_computation.6 | loop fusion | flops 3145728 | bytes 10518528 | tf_op jit(solution)/shard_map/convert_element_type | solution.py:38
  212.2 0.0 all-gather.2.cloned.1.call-done
  212.2 6.4 %convolution_convert_fusion = bf16[256,1024]{1,0:T(8,128)(2,1)S(1)} fusion(bf16[4096,256]{0,1:T(8,128)(2,1)} %fusion, bf16[1024,4096]{1,0:T(8,128)(2,1)} %all-gather.2.cloned.1.call-done), kind=kOutput, calls=%fused_computation.8 | convolution fusion | flops 2147745792 | bytes 11010048 | tf_op jit(solution)/shard_map/dot_general | solution.py:39
  218.6 0.0 copy-done
  218.6 1.7 convolution_bitcast_fusion.1
  220.3 0.0 reduce-scatter.2.cloned.1.call-update
  220.4 0.3 copy.23
  220.6 0.1 broadcast_in_dim.42
  220.8 0.7 scatter_fusion
  221.5 1.2 copy.24
  222.7 2.3 copy.27
  225.0 24.7 %reduce-scatter.2.cloned.1.call-done = f32[256,256]{0,1:T(8,128)} async-done(((f32[1024,256]{0,1:T(8,128)}), f32[256,256]{0,1:T(8,128)}) %reduce-scatter.2.cloned.1.call-update) | async-done | bytes 262160 | tf_op jit(solution)/shard_map/reduce_scatter | solution.py:46
  249.7 1.0 convert_element_type.21
  250.6 0.1 copy.25
  250.8 0.6 scatter_fusion.1
  251.4 0.1 copy.26
  251.6 0.8 copy.28
  (5 shorter events, 0.0 us)
Async XLA Ops:
  7.2 211.4 %copy-start = (bf16[1024,1024]{1,0:T(8,128)(2,1)S(1)}, bf16[1024,1024]{1,0:T(8,128)(2,1)}, u32[]{:S(2)}) copy-start(bf16[1024,1024]{1,0:T(8,128)(2,1)} %param.15) | copy-start | bytes 6291460
  7.2 205.0 %all-gather.2.cloned.1.call-start = ((), (), s32[]{:S(2)}) async-start(), calls=%async_computation.1 | async-start | bytes 9437184 | tf_op jit(solution)/shard_map/all_gather | solution.py:40
  7.9 241.8 %reduce-scatter.2.cloned.1.call-start = ((), (), s32[]{:S(2)}) async-start(), calls=%async_computation.2 | async-start | bytes 1310720 | tf_op jit(solution)/shard_map/reduce_scatter | solution.py:46
  18.5 97.9 %copy-start.2 = (s32[3]{0:T(128)S(1)}, s32[3]{0:T(128)}, u32[]{:S(2)}) copy-start(s32[3]{0:T(128)} %param.12) | copy-start | bytes 40
  18.5 98.5 %copy-start.1 = (f32[4096]{0:T(1024)S(1)}, f32[4096]{0:T(1024)}, u32[]{:S(2)}) copy-start(f32[4096]{0:T(1024)} %param.10) | copy-start | bytes 49156
  18.5 98.5 %copy-start.3 = (f32[20]{0:T(128)S(1)}, f32[20]{0:T(128)}, u32[]{:S(2)}) copy-start(f32[20]{0:T(128)} %param.11) | copy-start | bytes 244
  18.5 93.6 %collective-permute-start = (f32[4096,256]{0,1:T(8,128)S(1)}, f32[4096,256]{0,1:T(8,128)S(1)}, u32[]{:S(2)}, u32[]{:S(2)}) collective-permute-start(f32[4096,256]{0,1:T(8,128)S(1)} %convolution_bitcast_fusion), channel_id=1, source_target_pairs={{0,8},{8,0},{16,24},{24,16},{1,9},{9,1},{17,25},{25,17},{2,10},{10... | collective-permute-start | bytes 12582920 | tf_op jit(solution)/shard_map/ppermute | solution.py:31
  114.6 92.1 %collective-permute-start.1 = (f32[4096,256]{0,1:T(8,128)}, f32[4096,256]{0,1:T(8,128)}, u32[]{:S(2)}, u32[]{:S(2)}) collective-permute-start(f32[4096,256]{0,1:T(8,128)} %add.34), channel_id=1, source_target_pairs={{0,16},{8,24},{16,0},{24,8},{1,17},{9,25},{17,1},{25,9},{2,18},{10... | collective-permute-start | bytes 12582920 | tf_op jit(solution)/shard_map/ppermute | solution.py:31
Sparse Core Ops, SparseCore 0:
  9.6 84.7 all-gather.1
  220.5 29.1 reduce-scatter.1
